TPU v7x, 32 devices: a whole 2x2x4 slice. The times are simulated.
32 devices in a mesh: grp: 4 (over y, core), node: 8 (over z, x).
Axes of the slice: x: 2, y: 2, z: 4, core: 2. Of those that a mesh axis runs over, the one named last changes fastest.
Arguments:
- excitation: float32 [128, 32768], P(None, ('grp', 'node')), may hold values from -6 to 6
- points: float32 [3, 32768], P(None, ('grp', 'node')), may hold values from -5 to 5
- near_mask: int32 [32, 2], P(('grp', 'node')), may hold values from 0 to 1, as said below
- bit_order: int32 [3], replicated, may hold values from 0 to 2, as said below
- compress: float32 [32768, 256], P(('grp', 'node')), may hold values from -0.1875 to 0.1875
- level_self: float32 [3, 8192, 256], P(None, ('grp', 'node')), may hold values from -0.25 to 0.25
- level_partner: float32 [3, 8192, 256], P(None, ('grp', 'node')), may hold values from -0.25 to 0.25
- expand: float32 [8192, 4096], P(('grp', 'node')), may hold values from -0.375 to 0.375
Outputs:
- field: float32 [128, 32768], P(None, ('grp', 'node'))
Inputs may be any that keep to these rules, and one draw needn't show every extreme that they name: near_mask[b, 0] is 0 when b is the first cluster of its group and near_mask[b, 1] is 0 when b is the last; otherwise each entry is 0 or 1. `bit_order`: the entries are distinct bits of a node index; each of 0 to 2 appears once.
All inputs are finite; a program needn't handle non-finite values.
Results may differ from a plain program's by a relative error of at most 0.0001.
Values sent between devices are 32-bit elements; how exact they have to be, the bound alone decides.
No kernel may reach another device: no remote copies, remote signals or barrier semaphores. Data moves between devices by JAX's collectives and lax.ppermute only.
A program may use at most 64 MiB of HBM per device.

v0:
```python
import functools
import math

import jax
import jax.numpy as jnp
from jax import lax
from jax.sharding import PartitionSpec as P

HIGH = lax.Precision.HIGHEST
SOFTEN = 0.01


def partner(block, axis, apart):
    count = lax.axis_size(axis)
    route = []
    for low in range(count):
        high = low | 1 << apart
        if high != low and high < count:
            route += [(low, high), (high, low)]
    return lax.ppermute(block, axis, route)


def padded(cells, sides, width):
    for axis, dim in sides:
        count = lax.axis_size(axis)
        ends = count - 1
        head = lax.slice_in_dim(cells, 0, width, axis=dim)
        tail = lax.slice_in_dim(cells, cells.shape[dim] - width, cells.shape[dim], axis=dim)
        cells = jnp.concatenate(
            [
                lax.ppermute(tail, axis, [(i, (i + 1) % count) for i in range(ends)]),
                cells,
                lax.ppermute(head, axis, [((i + 1) % count, i) for i in range(ends)]),
            ],
            axis=dim,
        )
    return cells


def kernel_block(sources, targets):
    dist_sq = (sources[0][:, None] - targets[0][None, :]) ** 2
    dist_sq = dist_sq + (sources[1][:, None] - targets[1][None, :]) ** 2
    dist_sq = dist_sq + (sources[2][:, None] - targets[2][None, :]) ** 2
    return lax.rsqrt(dist_sq + SOFTEN) * (1.0 / math.sqrt(sources.shape[1]))


def partner_state(value, bit):
    return partner(value, "node", bit)


def shards(excitation, points, near_mask, bit_order, compress, level_self, level_partner, expand):
    width = excitation.shape[1]
    state = jnp.dot(excitation, compress, precision=HIGH)
    bit_count = lax.axis_size("node").bit_length() - 1
    branches = [functools.partial(partner_state, bit=bit) for bit in range(bit_count)]
    for level in range(level_self.shape[0]):
        own_part = jnp.dot(state, level_self[level], precision=HIGH)
        moved = lax.switch(bit_order[level], branches, state)
        state = own_part + jnp.dot(moved, level_partner[level], precision=HIGH)
    partial_far = jnp.dot(state, expand, precision=HIGH)
    far = lax.psum_scatter(partial_far, "grp", scatter_dimension=1, tiled=True)
    wide_x, wide_p = (
        padded(excitation, (("node", 1),), width),
        padded(points, (("node", 1),), width),
    )
    flags = near_mask[0].astype(jnp.float32)

    def near_term(which):
        src_x = wide_x[:, which * width : (which + 1) * width]
        src_p = wide_p[:, which * width : (which + 1) * width]
        return jnp.dot(src_x, kernel_block(src_p, points), precision=HIGH)

    near = near_term(1)
    near = near + flags[0] * near_term(0) + flags[1] * near_term(2)
    return far + near


def solution(mesh):
    return jax.shard_map(
        shards,
        mesh=mesh,
        in_specs=(
            P(None, ("grp", "node")),
            P(None, ("grp", "node")),
            P(("grp", "node"), None),
            P(),
            P(("grp", "node"), None),
            P(None, ("grp", "node"), None),
            P(None, ("grp", "node"), None),
            P(("grp", "node"), None),
        ),
        out_specs=P(None, ("grp", "node")),
        check_vma=False,
    )
```

profile of v0, /device:TPU:0, one launch (start us, length us, event | category | flops | bytes accessed | tf_op | source)
XLA Modules:
  0.0 90.4 jit_solution(7756422440361844731)
XLA Ops:
  6.5 0.0 copy-start
  6.5 0.0 reduce-scatter.2.cloned.1.call-start
  6.5 1.4 %fusion.103 = (s32[1]{0:T(128)}, s32[1]{0:T(128)}, s32[1]{0:T(128)}) fusion(s32[3]{0:T(128)} %param.20), kind=kLoop, calls=%fused_computation.94 | loop fusion | bytes 24 | tf_op jit(solution)/shard_map/slice | solution.py:58
  8.0 0.0 copy-done
  8.0 1.7 %fusion.104 = f32[128,256]{1,0:T(8,128)S(1)} fusion(f32[128,1024]{1,0:T(8,128)} %param.17, f32[1024,256]{1,0:T(8,128)S(1)} %copy-done), kind=kOutput, calls=%fused_computation.95 | convolution fusion | flops 402653184 | bytes 1703936 | tf_op jit(solution)/shard_map/dot_general | solution.py:53
  9.7 1.2 %fusion.85 = f32[128,256]{1,0:T(8,128)S(1)} fusion(f32[128,256]{1,0:T(8,128)S(1)} %fusion.104, f32[3,256,256]{2,1,0:T(8,128)} %param.22), kind=kOutput, calls=%fused_computation.76 | convolution fusion | flops 100663296 | bytes 524288 | tf_op jit(solution)/shard_map/dot_general | solution.py:57
  11.6 6.7 %conditional.3 = (f32[128,256]{1,0:T(8,128)}) conditional(s32[]{:T(128)} %bitcast.1, f32[128,256]{1,0:T(8,128)S(1)} %fusion.104, f32[128,256]{1,0:T(8,128)S(1)} %fusion.104, f32[128,256]{1,0:T(8,128)S(1)} %fusion.104), branch_computations={%region_0.0_spmd, %region_1.0_spmd, %region_2.0_spmd} | conditional | bytes 524336 | solution.py:58
  11.6 3.1 %collective-permute-start.1 = (f32[128,256]{1,0:T(8,128)S(1)}, f32[128,256]{1,0:T(8,128)}, u32[]{:S(2)}, u32[]{:S(2)}) collective-permute-start(f32[128,256]{1,0:T(8,128)S(1)} %param.1), channel_id=1, source_target_pairs={{0,2},{2,0},{1,3},{3,1},{4,6},{6,4},{5,7},{7,5},{8,10},{10,8},{9,1... | collective-permute-start | bytes 393224 | tf_op jit(solution)/shard_map/cond/branch_1_fun/ppermute | solution.py:20
  14.7 3.6 %collective-permute-done.1 = f32[128,256]{1,0:T(8,128)} collective-permute-done((f32[128,256]{1,0:T(8,128)S(1)}, f32[128,256]{1,0:T(8,128)}, u32[]{:S(2)}, u32[]{:S(2)}) %collective-permute-start.1) | collective-permute-done | bytes 131104 | tf_op jit(solution)/shard_map/cond/branch_1_fun/ppermute | solution.py:20
  18.3 1.3 %convolution_add_fusion.2 = f32[128,256]{1,0:T(8,128)S(1)} fusion(f32[128,256]{1,0:T(8,128)S(1)} %fusion.85, f32[128,256]{1,0:T(8,128)} %get-tuple-element.40, f32[3,256,256]{2,1,0:T(8,128)} %param.23), kind=kOutput, calls=%fused_computation.68 | convolution fusion | flops 100696064 | bytes 655360 | tf_op jit(solution)/shard_map/dot_general | solution.py:59
  19.6 1.2 %fusion.82 = f32[128,256]{1,0:T(8,128)S(1)} fusion(f32[128,256]{1,0:T(8,128)S(1)} %convolution_add_fusion.2, f32[3,256,256]{2,1,0:T(8,128)} %param.22), kind=kOutput, calls=%fused_computation.73 | convolution fusion | flops 100663296 | bytes 524288 | tf_op jit(solution)/shard_map/dot_general | solution.py:57
  21.5 5.2 %conditional.4 = (f32[128,256]{1,0:T(8,128)}) conditional(s32[]{:T(128)} %bitcast.4, f32[128,256]{1,0:T(8,128)S(1)} %convolution_add_fusion.2, f32[128,256]{1,0:T(8,128)S(1)} %convolution_add_fusion.2, f32[128,256]{1,0:T(8,128)S(1)} %convolution_add_fusion.2), branch_computations={%region_3.0_spmd, %region_4.0_spmd, %region_5.0_spmd} | conditional | bytes 524336 | solution.py:58
  21.5 1.7 %collective-permute-start.3 = (f32[128,256]{1,0:T(8,128)S(1)}, f32[128,256]{1,0:T(8,128)}, u32[]{:S(2)}, u32[]{:S(2)}) collective-permute-start(f32[128,256]{1,0:T(8,128)S(1)} %param.3), channel_id=1, source_target_pairs={{0,1},{1,0},{2,3},{3,2},{4,5},{5,4},{6,7},{7,6},{8,9},{9,8},{10,11... | collective-permute-start | bytes 393224 | tf_op jit(solution)/shard_map/cond/branch_0_fun/ppermute | solution.py:20
  23.2 3.4 %collective-permute-done.3 = f32[128,256]{1,0:T(8,128)} collective-permute-done((f32[128,256]{1,0:T(8,128)S(1)}, f32[128,256]{1,0:T(8,128)}, u32[]{:S(2)}, u32[]{:S(2)}) %collective-permute-start.3) | collective-permute-done | bytes 131104 | tf_op jit(solution)/shard_map/cond/branch_0_fun/ppermute | solution.py:20
  26.7 1.3 %convolution_add_fusion.1 = f32[128,256]{1,0:T(8,128)S(1)} fusion(f32[128,256]{1,0:T(8,128)S(1)} %fusion.82, f32[128,256]{1,0:T(8,128)} %get-tuple-element.41, f32[3,256,256]{2,1,0:T(8,128)} %param.23), kind=kOutput, calls=%fused_computation.67 | convolution fusion | flops 100696064 | bytes 655360 | tf_op jit(solution)/shard_map/dot_general | solution.py:59
  28.0 1.2 %fusion.79 = f32[128,256]{1,0:T(8,128)S(1)} fusion(f32[128,256]{1,0:T(8,128)S(1)} %convolution_add_fusion.1, f32[3,256,256]{2,1,0:T(8,128)} %param.22), kind=kOutput, calls=%fused_computation.70 | convolution fusion | flops 100663296 | bytes 524288 | tf_op jit(solution)/shard_map/dot_general | solution.py:57
  29.9 7.5 %conditional.5 = (f32[128,256]{1,0:T(8,128)}) conditional(s32[]{:T(128)} %bitcast.7, f32[128,256]{1,0:T(8,128)S(1)} %convolution_add_fusion.1, f32[128,256]{1,0:T(8,128)S(1)} %convolution_add_fusion.1, f32[128,256]{1,0:T(8,128)S(1)} %convolution_add_fusion.1), branch_computations={%region_6.0_spmd, %region_7.0_spmd, %region_8.0_spmd} | conditional | bytes 524336 | solution.py:58
  29.9 2.8 %collective-permute-start.8 = (f32[128,256]{1,0:T(8,128)S(1)}, f32[128,256]{1,0:T(8,128)}, u32[]{:S(2)}, u32[]{:S(2)}) collective-permute-start(f32[128,256]{1,0:T(8,128)S(1)} %param.8), channel_id=1, source_target_pairs={{0,4},{4,0},{1,5},{5,1},{2,6},{6,2},{3,7},{7,3},{8,12},{12,8},{9,1... | collective-permute-start | bytes 393224 | tf_op jit(solution)/shard_map/cond/branch_2_fun/ppermute | solution.py:20
  32.7 4.6 %collective-permute-done.8 = f32[128,256]{1,0:T(8,128)} collective-permute-done((f32[128,256]{1,0:T(8,128)S(1)}, f32[128,256]{1,0:T(8,128)}, u32[]{:S(2)}, u32[]{:S(2)}) %collective-permute-start.8) | collective-permute-done | bytes 131104 | tf_op jit(solution)/shard_map/cond/branch_2_fun/ppermute | solution.py:20
  37.3 1.3 %convolution_add_fusion = f32[128,256]{1,0:T(8,128)S(1)} fusion(f32[128,256]{1,0:T(8,128)S(1)} %fusion.79, f32[128,256]{1,0:T(8,128)} %get-tuple-element.42, f32[3,256,256]{2,1,0:T(8,128)} %param.23), kind=kOutput, calls=%fused_computation.66 | convolution fusion | flops 100696064 | bytes 655360 | tf_op jit(solution)/shard_map/dot_general | solution.py:59
  38.6 0.0 copy-start.1
  38.6 0.0 copy-start.2
  38.7 0.0 copy-start.3
  38.7 5.9 %fusion.105 = f32[128,4096]{1,0:T(8,128)} fusion(f32[128,256]{1,0:T(8,128)S(1)} %convolution_add_fusion, f32[256,4096]{1,0:T(8,128)} %param.24), kind=kOutput, calls=%fused_computation.96 | convolution fusion | flops 1610612736 | bytes 6422528 | tf_op jit(solution)/shard_map/dot_general | solution.py:60
  44.5 0.0 reduce-scatter.2.cloned.1.call-update
  44.6 0.0 copy-done.1
  44.6 3.6 %collective-permute-start.10 = (f32[128,1024]{1,0:T(8,128)S(1)}, f32[128,1024]{1,0:T(8,128)S(1)}, u32[]{:S(2)}, u32[]{:S(2)}) collective-permute-start(f32[128,1024]{1,0:T(8,128)S(1)} %copy-done.1), channel_id=1, source_target_pairs={{0,1},{1,2},{2,3},{3,4},{4,5},{5,6},{6,7},{8,9},{9,10},{10,11},{11... | collective-permute-start | bytes 1572872 | tf_op jit(solution)/shard_map/ppermute | solution.py:31
  48.2 1.3 %collective-permute-start.12 = (f32[128,1024]{1,0:T(8,128)S(1)}, f32[128,1024]{1,0:T(8,128)S(1)}, u32[]{:S(2)}, u32[]{:S(2)}) collective-permute-start(f32[128,1024]{1,0:T(8,128)S(1)} %copy-done.1), channel_id=1, source_target_pairs={{1,0},{2,1},{3,2},{4,3},{5,4},{6,5},{7,6},{9,8},{10,9},{11,10},{12... | collective-permute-start | bytes 1572872 | tf_op jit(solution)/shard_map/ppermute | solution.py:33
  49.5 0.0 copy-done.2
  49.5 4.5 %collective-permute-start.9 = (f32[3,1024]{1,0:T(4,128)S(1)}, f32[3,1024]{1,0:T(4,128)S(1)}, u32[]{:S(2)}, u32[]{:S(2)}) collective-permute-start(f32[3,1024]{1,0:T(4,128)S(1)} %copy-done.2), channel_id=1, source_target_pairs={{0,1},{1,2},{2,3},{3,4},{4,5},{5,6},{6,7},{8,9},{9,10},{10,11},{11... | collective-permute-start | bytes 36872 | tf_op jit(solution)/shard_map/ppermute | solution.py:31
  54.0 1.5 %collective-permute-start.11 = (f32[3,1024]{1,0:T(4,128)S(1)}, f32[3,1024]{1,0:T(4,128)S(1)}, u32[]{:S(2)}, u32[]{:S(2)}) collective-permute-start(f32[3,1024]{1,0:T(4,128)S(1)} %copy-done.2), channel_id=1, source_target_pairs={{1,0},{2,1},{3,2},{4,3},{5,4},{6,5},{7,6},{9,8},{10,9},{11,10},{12... | collective-permute-start | bytes 36872 | tf_op jit(solution)/shard_map/ppermute | solution.py:33
  55.5 0.0 copy-done.3
  55.5 4.0 %fusion.24 = f32[1024,128]{0,1:T(8,128)S(1)} fusion(f32[128,1024]{1,0:T(8,128)S(1)} %copy-done.1, f32[1024]{0:T(1024)S(1)} %bitcast.52, f32[1024]{0:T(1024)S(1)} %bitcast.55, f32[1024]{0:T(1024)S(1)} %bitcast.49), kind=kOutput, calls=%fused_computation.24 | convolution fusion | flops 1621098496 | bytes 1060864 | tf_op jit(solution)/shard_map/dot_general | solution.py:71
  59.5 0.6 fusion.102
  60.1 8.0 %collective-permute-done.9 = f32[3,1024]{1,0:T(4,128)S(1)} collective-permute-done((f32[3,1024]{1,0:T(4,128)S(1)}, f32[3,1024]{1,0:T(4,128)S(1)}, u32[]{:S(2)}, u32[]{:S(2)}) %collective-permute-start.9) | collective-permute-done | bytes 12320 | tf_op jit(solution)/shard_map/ppermute | solution.py:31
  68.1 0.0 collective-permute-done.11
  68.1 0.0 collective-permute-done.10
  68.1 4.7 %fusion.75 = f32[1024,128]{0,1:T(8,128)S(1)} fusion(f32[1024,128]{0,1:T(8,128)S(1)} %fusion.24, f32[128,1024]{1,0:T(8,128)S(1)} %collective-permute-done.10, f32[1024]{0:T(1024)S(1)} %bitcast.62, f32[1024]{0:T(1024)S(1)} %bitcast.63, f32[1024]{0:T(1024)S(1)} %bitcast.61, f32[1024]{0:T(1024)S(1)} %bitcast.53, f32[1024]{0:T(1024)S(1)} %bitcast.56, ...), kind=kOutput, calls=%fused_computation.65 | convolution fusion | flops 1621360640 | bytes 1597444 | tf_op jit(solution)/shard_map/dot_general | solution.py:71
  72.8 0.0 collective-permute-done.12
  72.8 4.4 %reduce-scatter.2.cloned.1.call-done = f32[128,1024]{1,0:T(8,128)} async-done(((f32[128,4096]{1,0:T(8,128)}), f32[128,1024]{1,0:T(8,128)}) %reduce-scatter.2.cloned.1.call-update) | async-done | bytes 524304 | tf_op jit(solution)/shard_map/reduce_scatter | solution.py:61
  77.2 6.4 %fusion.72 = f32[128,1024]{1,0:T(8,128)} fusion(f32[128,1024]{1,0:T(8,128)} %reduce-scatter.2.cloned.1.call-done, f32[1024,128]{0,1:T(8,128)S(1)} %fusion.75, f32[128,1024]{1,0:T(8,128)S(1)} %collective-permute-done.12, f32[1024]{0:T(1024)S(1)} %bitcast.59, f32[1024]{0:T(1024)S(1)} %bitcast.60, f32[1024]{0:T(1024)S(1)} %bitcast.58, f32[1024]{0:T(1024)S(1)} %bitcast.54, ...), kind=kOutput, calls=%fused_computation.64 | convolution fusion | flops 1621491712 | bytes 2121732 | tf_op jit(solution)/shard_map/dot_general | solution.py:71
  (4 shorter events, 0.0 us)
Async XLA Ops:
  6.5 1.4 %copy-start = (f32[1024,256]{1,0:T(8,128)S(1)}, f32[1024,256]{1,0:T(8,128)}, u32[]{:S(2)}) copy-start(f32[1024,256]{1,0:T(8,128)} %param.21) | copy-start | bytes 3145732
  6.5 70.6 %reduce-scatter.2.cloned.1.call-start = ((), (), s32[]{:S(2)}) async-start(), calls=%async_computation.1 | async-start | bytes 2621440 | tf_op jit(solution)/shard_map/reduce_scatter | solution.py:61
  11.6 6.7 %collective-permute-start.1 = (f32[128,256]{1,0:T(8,128)S(1)}, f32[128,256]{1,0:T(8,128)}, u32[]{:S(2)}, u32[]{:S(2)}) collective-permute-start(f32[128,256]{1,0:T(8,128)S(1)} %param.1), channel_id=1, source_target_pairs={{0,2},{2,0},{1,3},{3,1},{4,6},{6,4},{5,7},{7,5},{8,10},{10,8},{9,1... | collective-permute-start | bytes 393224 | tf_op jit(solution)/shard_map/cond/branch_1_fun/ppermute | solution.py:20
  21.5 5.1 %collective-permute-start.3 = (f32[128,256]{1,0:T(8,128)S(1)}, f32[128,256]{1,0:T(8,128)}, u32[]{:S(2)}, u32[]{:S(2)}) collective-permute-start(f32[128,256]{1,0:T(8,128)S(1)} %param.3), channel_id=1, source_target_pairs={{0,1},{1,0},{2,3},{3,2},{4,5},{5,4},{6,7},{7,6},{8,9},{9,8},{10,11... | collective-permute-start | bytes 393224 | tf_op jit(solution)/shard_map/cond/branch_0_fun/ppermute | solution.py:20
  29.9 7.4 %collective-permute-start.8 = (f32[128,256]{1,0:T(8,128)S(1)}, f32[128,256]{1,0:T(8,128)}, u32[]{:S(2)}, u32[]{:S(2)}) collective-permute-start(f32[128,256]{1,0:T(8,128)S(1)} %param.8), channel_id=1, source_target_pairs={{0,4},{4,0},{1,5},{5,1},{2,6},{6,2},{3,7},{7,3},{8,12},{12,8},{9,1... | collective-permute-start | bytes 393224 | tf_op jit(solution)/shard_map/cond/branch_2_fun/ppermute | solution.py:20
  38.6 5.9 %copy-start.1 = (f32[128,1024]{1,0:T(8,128)S(1)}, f32[128,1024]{1,0:T(8,128)}, u32[]{:S(2)}) copy-start(f32[128,1024]{1,0:T(8,128)} %param.17) | copy-start | bytes 1572868
  38.6 10.8 %copy-start.2 = (f32[3,1024]{1,0:T(4,128)S(1)}, f32[3,1024]{1,0:T(4,128)}, u32[]{:S(2)}) copy-start(f32[3,1024]{1,0:T(4,128)} %param.18) | copy-start | bytes 36868
  38.7 16.9 %copy-start.3 = (s32[1,2]{1,0:T(1,128)S(1)}, s32[1,2]{1,0:T(1,128)}, u32[]{:S(2)}) copy-start(s32[1,2]{1,0:T(1,128)} %param.19) | copy-start | bytes 28
  44.6 23.6 %collective-permute-start.10 = (f32[128,1024]{1,0:T(8,128)S(1)}, f32[128,1024]{1,0:T(8,128)S(1)}, u32[]{:S(2)}, u32[]{:S(2)}) collective-permute-start(f32[128,1024]{1,0:T(8,128)S(1)} %copy-done.1), channel_id=1, source_target_pairs={{0,1},{1,2},{2,3},{3,4},{4,5},{5,6},{6,7},{8,9},{9,10},{10,11},{11... | collective-permute-start | bytes 1572872 | tf_op jit(solution)/shard_map/ppermute | solution.py:31
  48.2 24.6 %collective-permute-start.12 = (f32[128,1024]{1,0:T(8,128)S(1)}, f32[128,1024]{1,0:T(8,128)S(1)}, u32[]{:S(2)}, u32[]{:S(2)}) collective-permute-start(f32[128,1024]{1,0:T(8,128)S(1)} %copy-done.1), channel_id=1, source_target_pairs={{1,0},{2,1},{3,2},{4,3},{5,4},{6,5},{7,6},{9,8},{10,9},{11,10},{12... | collective-permute-start | bytes 1572872 | tf_op jit(solution)/shard_map/ppermute | solution.py:33
  49.5 18.6 %collective-permute-start.9 = (f32[3,1024]{1,0:T(4,128)S(1)}, f32[3,1024]{1,0:T(4,128)S(1)}, u32[]{:S(2)}, u32[]{:S(2)}) collective-permute-start(f32[3,1024]{1,0:T(4,128)S(1)} %copy-done.2), channel_id=1, source_target_pairs={{0,1},{1,2},{2,3},{3,4},{4,5},{5,6},{6,7},{8,9},{9,10},{10,11},{11... | collective-permute-start | bytes 36872 | tf_op jit(solution)/shard_map/ppermute | solution.py:31
  54.0 14.1 %collective-permute-start.11 = (f32[3,1024]{1,0:T(4,128)S(1)}, f32[3,1024]{1,0:T(4,128)S(1)}, u32[]{:S(2)}, u32[]{:S(2)}) collective-permute-start(f32[3,1024]{1,0:T(4,128)S(1)} %copy-done.2), channel_id=1, source_target_pairs={{1,0},{2,1},{3,2},{4,3},{5,4},{6,5},{7,6},{9,8},{10,9},{11,10},{12... | collective-permute-start | bytes 36872 | tf_op jit(solution)/shard_map/ppermute | solution.py:33
Sparse Core Ops, SparseCore 0:
  44.7 32.4 reduce-scatter.1
where the time goes:
time: 90.9 us; the launch traced here: 90.4 us
  matrix products  30.1 us (33%)
  waiting for transfers between devices  24 us (26%)
  starting transfers between devices  18.5 us (20%)
  between operations  15.6 us (17%)
  local copies, waits for them, and re-layouts  2.06 us (2%)
    dot_general x3, matrix products, near_term(): return jnp.dot(src_x, kernel_block(src_p, points), precision=HIGH)  15 us
    ppermute x3, waiting for transfers between devices, partner(): return lax.ppermute(block, axis, route)  11.7 us
    ppermute x2, starting transfers between devices, padded(): lax.ppermute(tail, axis, [(i, (i + 1) % count) for i in range(ends)])  8.13 us
    ppermute x2, waiting for transfers between devices, padded(): lax.ppermute(tail, axis, [(i, (i + 1) % count) for i in range(ends)])  8 us
    ppermute x3, starting transfers between devices, partner(): return lax.ppermute(block, axis, route)  7.65 us
    dot_general x1, matrix products, shards(): partial_far = jnp.dot(state, expand, precision=HIGH)  5.86 us
    reduce_scatter x1, waiting for transfers between devices, shards(): far = lax.psum_scatter(partial_far, 'grp', scatter_dimension=1, tiled=True)  4.37 us
    dot_general x3, matrix products, shards(): state = own_part + jnp.dot(moved, level_partner[level], precision=HIGH)  3.9 us
  transfers between devices with their start and end apart: 8, of which 5 were waited for; matrix products, arithmetic and copies ran while one was open for 10% of the time, Pallas kernels for 0%

commit v1 on v0

v1 whole, which is shorter than its diff:
```python
import functools
import itertools
import math

import jax
import jax.numpy as jnp
from jax import lax
from jax.sharding import PartitionSpec as P

HIGH = lax.Precision.HIGH
SOFTEN = 0.01
MOST_ORDERS = 6


def swapped(block, axis, bit):
    count = lax.axis_size(axis)
    return lax.ppermute(block, axis, [(i, i ^ 1 << bit) for i in range(count) if i ^ 1 << bit < count])


def dot(left, right):
    return jnp.dot(left, right, precision=HIGH)


def kernel_block(sources, targets):
    dist_sq = (sources[0][:, None] - targets[0][None, :]) ** 2
    dist_sq = dist_sq + (sources[1][:, None] - targets[1][None, :]) ** 2
    dist_sq = dist_sq + (sources[2][:, None] - targets[2][None, :]) ** 2
    return lax.rsqrt(dist_sq + SOFTEN) * (1.0 / math.sqrt(sources.shape[1]))


def level_step(state, own, other, bit):
    moved = swapped(state, "node", bit)
    return dot(state, own) + dot(moved, other)


def butterfly(state, level_self, level_partner, bit_order):
    levels = level_self.shape[0]
    bits = lax.axis_size("node").bit_length() - 1
    orders = list(itertools.permutations(range(bits), levels))
    if len(orders) > MOST_ORDERS:
        for level in range(levels):
            steps = [functools.partial(level_step, bit=bit) for bit in range(bits)]
            state = lax.switch(bit_order[level], steps, state, level_self[level], level_partner[level])
        return state

    def whole(order):
        def run(state):
            for level, bit in enumerate(order):
                state = level_step(state, level_self[level], level_partner[level], bit)
            return state

        return run

    which = sum(
        jnp.all(bit_order == jnp.array(order, jnp.int32)).astype(jnp.int32) * at
        for at, order in enumerate(orders)
    )
    return lax.switch(which, [whole(order) for order in orders], state)


def shards(excitation, points, near_mask, bit_order, compress, level_self, level_partner, expand):
    cols, width = excitation.shape
    rank = compress.shape[1]
    nodes, groups = lax.axis_size("node"), lax.axis_size("grp")
    node, group = lax.axis_index("node"), lax.axis_index("grp")
    flags = near_mask[0].astype(jnp.float32)

    packed = jnp.concatenate([excitation, points], axis=0)
    first = swapped(packed, "node", 0)
    route = [(i, i + 2) for i in range(0, nodes - 2, 2)] + [(i, i - 2) for i in range(3, nodes, 2)]
    second = lax.ppermute(first, "node", route)
    odd = node % 2
    first_flag = jnp.where(odd == 1, flags[0], flags[1])
    second_flag = jnp.where(odd == 1, flags[1], flags[0])

    other_expand = swapped(expand, "grp", 0)

    state = dot(excitation, compress)
    state = butterfly(state, level_self, level_partner, bit_order)
    other_state = swapped(state, "grp", 0)

    def share(target):
        own_cols = lax.dynamic_slice_in_dim(expand, target * width, width, axis=1)
        other_cols = lax.dynamic_slice_in_dim(other_expand, target * width, width, axis=1)
        return dot(state, own_cols) + dot(other_state, other_cols)

    apart = groups // 2
    total = None
    ring = groups // 2
    bits = ring.bit_length() - 1
    held = [share(group ^ (k << 1)) for k in reversed(range(ring))]
    held = held[::-1]
    for bit in reversed(range(bits)):
        half = 1 << bit
        away = held[half:]
        held = held[:half]
        got = [swapped(piece, "grp", bit + 1) for piece in away]
        held = [a + b for a, b in zip(held, got)]
    far = held[0]

    def near_term(block, flag):
        return dot(block[:cols] * flag, kernel_block(block[cols:], points))

    near = dot(excitation, kernel_block(points, points))
    near = near + near_term(first, first_flag) + near_term(second, second_flag)
    return far + near


def solution(mesh):
    return jax.shard_map(
        shards,
        mesh=mesh,
        in_specs=(
            P(None, ("grp", "node")),
            P(None, ("grp", "node")),
            P(("grp", "node"), None),
            P(),
            P(("grp", "node"), None),
            P(None, ("grp", "node"), None),
            P(None, ("grp", "node"), None),
            P(("grp", "node"), None),
        ),
        out_specs=P(None, ("grp", "node")),
        check_vma=False,
    )
```

time: 90.9 us -> 71.5 us (0.79)
  between operations: 15.6 us -> 6.01 us
  matrix products: 30.1 us -> 25.2 us
  starting transfers between devices: 18.5 us -> 13.7 us
  other arithmetic: 0.01 us -> 1.57 us
  waiting for transfers between devices: 24 us -> 22.7 us
    dot_general x11 -> x14, matrix products: 30.1 us -> 25.2 us  [dot(): return jnp.dot(left, right, precision=HIGH)]
    ppermute x7 -> x8, starting transfers between devices: 18.5 us -> 13.7 us  [the longest x7 10.6 us: swapped(): lax.ppermute(block, axis, [(i, i ^ 1 << bit) for i in range(count) if i ^...]
    reduce_scatter x1 -> x0, waiting for transfers between devices: 4.37 us -> none  [shards(): far = lax.psum_scatter(partial_far, 'grp', scatter_dimension=1, tiled=True)]
    ppermute x7 -> x8, waiting for transfers between devices: 19.7 us -> 22.7 us  [the longest x7 18.9 us: swapped(): lax.ppermute(block, axis, [(i, i ^ 1 << bit) for i in range(count) if i ^...]
    reduce_and x0 -> x1, other arithmetic: none -> 1.53 us  [butterfly(): jnp.all(bit_order == jnp.array(order, jnp.int32)).astype(jnp.int32) * at]
    slice x2 -> x1, local copies, waits for them, and re-layouts: 2.01 us -> 0.58 us  [shards(): first_flag = jnp.where(odd == 1, flags[0], flags[1])]
  transfers between devices with their start and end apart: 8 -> 8, of which waited for: 5 -> 6; matrix products, arithmetic and copies ran while one was open for 10% -> 32% of each run, Pallas kernels for 0% -> 0%
where the time goes in v1:
time: 71.5 us; the launch traced here: 70.8 us
  matrix products  25.2 us (35%)
  waiting for transfers between devices  22.7 us (32%)
  starting transfers between devices  13.7 us (19%)
  between operations  6.01 us (8%)
  other arithmetic  1.57 us (2%)
  local copies, waits for them, and re-layouts  1.51 us (2%)
    dot_general x14, matrix products, dot(): return jnp.dot(left, right, precision=HIGH)  25.2 us
    ppermute x7, waiting for transfers between devices, swapped(): lax.ppermute(block, axis, [(i, i ^ 1 << bit) for i in range(count) if i ^...  18.9 us
    ppermute x7, starting transfers between devices, swapped(): lax.ppermute(block, axis, [(i, i ^ 1 << bit) for i in range(count) if i ^...  10.6 us
    ppermute x1, waiting for transfers between devices, shards(): second = lax.ppermute(first, 'node', route)  3.79 us
    ppermute x1, starting transfers between devices, shards(): second = lax.ppermute(first, 'node', route)  3.11 us
    reduce_and x1, other arithmetic, butterfly(): jnp.all(bit_order == jnp.array(order, jnp.int32)).astype(jnp.int32) * at  1.53 us
  transfers between devices with their start and end apart: 8, of which 6 were waited for; matrix products, arithmetic and copies ran while one was open for 32% of the time, Pallas kernels for 0%

profile of v1, /device:TPU:0, one launch (start us, length us, event | category | flops | bytes accessed | tf_op | source)
XLA Modules:
  0.0 70.8 jit_solution(17279162188091440521)
XLA Ops:
  0.0 0.0 copy-start
  0.0 0.5 collective-permute-start.19
  0.5 1.5 %compare_reduce_fusion = (pred[]{:T(512)}, pred[]{:T(512)}, pred[]{:T(512)}, pred[]{:T(512)}, pred[]{:T(512)}) fusion(s32[3]{0:T(128)} %param.22, s32[3]{0:T(128)} %constant.59.clone, s32[3]{0:T(128)} %constant.57.clone, s32[3]{0:T(128)} %constant.56.clone, s32[3]{0:T(128)} %constant.55.clone, s32[3]{0:T(128)} %constant.58.clone), kind=kLoop, calls=%fused_computation.186 | loop fusion | flops 25 | bytes 77 | tf_op jit(solution)/shard_map/reduce_and | solution.py:55
  5.3 0.0 copy-done
  5.3 1.5 %fusion.185 = f32[128,256]{1,0:T(8,128)S(1)} fusion(f32[128,1024]{1,0:T(8,128)} %param.19, f32[1024,256]{1,0:T(8,128)S(1)} %copy-done), kind=kOutput, calls=%fused_computation.205 | convolution fusion | flops 201326592 | bytes 1703936 | tf_op jit(solution)/shard_map/dot_general | solution.py:21
  6.8 0.0 copy-start.1
  6.8 0.0 copy-start.2
  6.8 0.0 copy-start.3
  6.8 24.4 %conditional.1 = (f32[128,256]{1,0:T(8,128)S(1)}) conditional(s32[]{:T(128)} %clamp.3, (f32[3,256,256]{2,1,0:T(8,128)}, f32[128,256]{1,0:T(8,128)S(1)}, f32[3,256,256]{2,1,0:T(8,128)}) %tuple.23, (f32[3,256,256]{2,1,0:T(8,128)}, f32[128,256]{1,0:T(8,128)S(1)}, f32[3,256,256]{2,1,0:T(8,128)}) %tuple.23, ...), branch_computations={%region_5.6_spmd, %region_6.7_spmd, %region_7.8_spmd, %region_8.9_... | conditional | flops 302088192 | bytes 5111936 | solution.py:58
  6.9 2.7 %collective-permute-start.9 = (f32[128,256]{1,0:T(8,128)S(1)}, f32[128,256]{1,0:T(8,128)S(1)}, u32[]{:S(2)}, u32[]{:S(2)}) collective-permute-start(f32[128,256]{1,0:T(8,128)S(1)} %get-tuple-element.57), channel_id=1, source_target_pairs={{0,2},{1,3},{2,0},{3,1},{4,6},{5,7},{6,4},{7,5},{8,10},{9,11},{10,... | collective-permute-start | bytes 393224 | tf_op jit(solution)/shard_map/cond/branch_3_fun/ppermute | solution.py:17
  9.6 1.2 %fusion.52 = f32[128,256]{1,0:T(8,128)S(1)} fusion(f32[128,256]{1,0:T(8,128)S(1)} %get-tuple-element.57, f32[3,256,256]{2,1,0:T(8,128)} %get-tuple-element.58), kind=kOutput, calls=%fused_computation.64 | convolution fusion | flops 50331648 | bytes 524288 | tf_op jit(solution)/shard_map/cond/branch_3_fun/dot_general | solution.py:21
  10.8 2.9 %collective-permute-done.9 = f32[128,256]{1,0:T(8,128)S(1)} collective-permute-done((f32[128,256]{1,0:T(8,128)S(1)}, f32[128,256]{1,0:T(8,128)S(1)}, u32[]{:S(2)}, u32[]{:S(2)}) %collective-permute-start.9) | collective-permute-done | bytes 131104 | tf_op jit(solution)/shard_map/cond/branch_3_fun/ppermute | solution.py:17
  13.7 1.2 %convolution_add_fusion.11 = f32[128,256]{1,0:T(8,128)S(1)} fusion(f32[128,256]{1,0:T(8,128)S(1)} %fusion.52, f32[128,256]{1,0:T(8,128)S(1)} %collective-permute-done.9, f32[3,256,256]{2,1,0:T(8,128)} %get-tuple-element.59), kind=kOutput, calls=%fused_computation.56 | convolution fusion | flops 50364416 | bytes 655360 | tf_op jit(solution)/shard_map/cond/branch_3_fun/dot_general | solution.py:21
  14.8 2.8 %collective-permute-start.10 = (f32[128,256]{1,0:T(8,128)S(1)}, f32[128,256]{1,0:T(8,128)S(1)}, u32[]{:S(2)}, u32[]{:S(2)}) collective-permute-start(f32[128,256]{1,0:T(8,128)S(1)} %convolution_add_fusion.11), channel_id=1, source_target_pairs={{0,4},{1,5},{2,6},{3,7},{4,0},{5,1},{6,2},{7,3},{8,12},{9,13},{10,... | collective-permute-start | bytes 393224 | tf_op jit(solution)/shard_map/cond/branch_3_fun/ppermute | solution.py:17
  17.7 1.2 %fusion.49 = f32[128,256]{1,0:T(8,128)S(1)} fusion(f32[128,256]{1,0:T(8,128)S(1)} %convolution_add_fusion.11, f32[3,256,256]{2,1,0:T(8,128)} %get-tuple-element.58), kind=kOutput, calls=%fused_computation.61 | convolution fusion | flops 50331648 | bytes 524288 | tf_op jit(solution)/shard_map/cond/branch_3_fun/dot_general | solution.py:21
  18.8 5.0 %collective-permute-done.10 = f32[128,256]{1,0:T(8,128)S(1)} collective-permute-done((f32[128,256]{1,0:T(8,128)S(1)}, f32[128,256]{1,0:T(8,128)S(1)}, u32[]{:S(2)}, u32[]{:S(2)}) %collective-permute-start.10) | collective-permute-done | bytes 131104 | tf_op jit(solution)/shard_map/cond/branch_3_fun/ppermute | solution.py:17
  23.9 1.2 %convolution_add_fusion.10 = f32[128,256]{1,0:T(8,128)S(1)} fusion(f32[128,256]{1,0:T(8,128)S(1)} %fusion.49, f32[128,256]{1,0:T(8,128)S(1)} %collective-permute-done.10, f32[3,256,256]{2,1,0:T(8,128)} %get-tuple-element.59), kind=kOutput, calls=%fused_computation.55 | convolution fusion | flops 50364416 | bytes 655360 | tf_op jit(solution)/shard_map/cond/branch_3_fun/dot_general | solution.py:21
  25.0 1.4 %collective-permute-start.11 = (f32[128,256]{1,0:T(8,128)S(1)}, f32[128,256]{1,0:T(8,128)S(1)}, u32[]{:S(2)}, u32[]{:S(2)}) collective-permute-start(f32[128,256]{1,0:T(8,128)S(1)} %convolution_add_fusion.10), channel_id=1, source_target_pairs={{0,1},{1,0},{2,3},{3,2},{4,5},{5,4},{6,7},{7,6},{8,9},{9,8},{10,11... | collective-permute-start | bytes 393224 | tf_op jit(solution)/shard_map/cond/branch_3_fun/ppermute | solution.py:17
  26.5 1.2 %fusion.46 = f32[128,256]{1,0:T(8,128)S(1)} fusion(f32[128,256]{1,0:T(8,128)S(1)} %convolution_add_fusion.10, f32[3,256,256]{2,1,0:T(8,128)} %get-tuple-element.58), kind=kOutput, calls=%fused_computation.58 | convolution fusion | flops 50331648 | bytes 524288 | tf_op jit(solution)/shard_map/cond/branch_3_fun/dot_general | solution.py:21
  27.7 2.4 %collective-permute-done.11 = f32[128,256]{1,0:T(8,128)S(1)} collective-permute-done((f32[128,256]{1,0:T(8,128)S(1)}, f32[128,256]{1,0:T(8,128)S(1)}, u32[]{:S(2)}, u32[]{:S(2)}) %collective-permute-start.11) | collective-permute-done | bytes 131104 | tf_op jit(solution)/shard_map/cond/branch_3_fun/ppermute | solution.py:17
  30.1 1.2 %convolution_add_fusion.9 = f32[128,256]{1,0:T(8,128)S(1)} fusion(f32[128,256]{1,0:T(8,128)S(1)} %fusion.46, f32[128,256]{1,0:T(8,128)S(1)} %collective-permute-done.11, f32[3,256,256]{2,1,0:T(8,128)} %get-tuple-element.59), kind=kOutput, calls=%fused_computation.54 | convolution fusion | flops 50364416 | bytes 655360 | tf_op jit(solution)/shard_map/cond/branch_3_fun/dot_general | solution.py:21
  31.3 0.1 collective-permute-start.18
  31.4 0.0 copy-done.1
  31.4 0.0 copy-done.2
  31.4 1.4 %collective-permute-start.21 = (f32[131,1024]{1,0:T(8,128)S(1)}, f32[131,1024]{1,0:T(8,128)}, u32[]{:S(2)}, u32[]{:S(2)}) collective-permute-start(f32[131,1024]{1,0:T(8,128)S(1)} %pad_maximum_fusion), channel_id=1, source_target_pairs={{0,1},{1,0},{2,3},{3,2},{4,5},{5,4},{6,7},{7,6},{8,9},{9,8},{10,11... | collective-permute-start | bytes 1609736 | tf_op jit(solution)/shard_map/ppermute | solution.py:17
  32.9 0.0 copy-done.3
  32.9 1.6 %fusion.164 = f32[128,1024]{1,0:T(8,128)S(1)} fusion(f32[128,256]{1,0:T(8,128)S(1)} %get-tuple-element.82, f32[256,4096]{1,0:T(8,128)} %param.26, s32[]{:T(128)S(6)} %select_n.23), kind=kOutput, calls=%fused_computation.176 | convolution fusion | flops 201326592 | bytes 1703940 | tf_op jit(solution)/shard_map/dot_general | solution.py:21
  34.5 1.6 %fusion.167 = f32[128,1024]{1,0:T(8,128)S(1)} fusion(f32[128,256]{1,0:T(8,128)S(1)} %get-tuple-element.82, f32[256,4096]{1,0:T(8,128)} %param.26, s32[]{:T(128)S(6)} %select_n.22), kind=kOutput, calls=%fused_computation.179 | convolution fusion | flops 201326592 | bytes 1703940 | tf_op jit(solution)/shard_map/dot_general | solution.py:21
  36.2 0.6 fusion.184
  39.3 2.7 %fusion.151 = f32[128,1024]{1,0:T(8,128)S(1)} fusion(f32[128,1024]{1,0:T(8,128)S(1)} %copy-done.1, f32[1024]{0:T(1024)S(1)} %bitcast.170, f32[1024]{0:T(1024)S(1)} %bitcast.167, f32[1024]{0:T(1024)S(1)} %bitcast.164), kind=kOutput, calls=%fused_computation.171 | convolution fusion | flops 815792128 | bytes 1060864 | tf_op jit(solution)/shard_map/dot_general | solution.py:21
  42.0 4.6 %collective-permute-done.21 = f32[131,1024]{1,0:T(8,128)} collective-permute-done((f32[131,1024]{1,0:T(8,128)S(1)}, f32[131,1024]{1,0:T(8,128)}, u32[]{:S(2)}, u32[]{:S(2)}) %collective-permute-start.21) | collective-permute-done | bytes 536608 | tf_op jit(solution)/shard_map/ppermute | solution.py:17
  46.6 3.1 %collective-permute-start.22 = (f32[131,1024]{1,0:T(8,128)}, f32[131,1024]{1,0:T(8,128)S(1)}, u32[]{:S(2)}, u32[]{:S(2)}) collective-permute-start(f32[131,1024]{1,0:T(8,128)} %collective-permute-done.21), channel_id=1, source_target_pairs={{0,2},{2,4},{4,6},{3,1},{5,3},{7,5},{8,10},{10,12},{12,14},{11,9},... | collective-permute-start | bytes 1609736 | tf_op jit(solution)/shard_map/ppermute | solution.py:71
  49.7 0.9 %fusion.182 = (f32[1,1024]{1,0:T(1,128)S(1)}, f32[1,1024]{1,0:T(1,128)S(1)}, f32[1,1024]{1,0:T(1,128)S(1)}) fusion(f32[131,1024]{1,0:T(8,128)} %collective-permute-done.21), kind=kLoop, calls=%fused_computation.202 | loop fusion | bytes 24576 | tf_op jit(solution)/shard_map/slice | solution.py:25
  50.6 0.0 collective-permute-done.18
  50.6 0.0 collective-permute-done.19
  50.6 1.6 %convolution_add_fusion.18 = f32[128,1024]{1,0:T(8,128)S(1)} fusion(f32[128,1024]{1,0:T(8,128)S(1)} %fusion.164, f32[128,256]{1,0:T(8,128)S(1)} %collective-permute-done.18, f32[256,4096]{1,0:T(8,128)} %collective-permute-done.19, s32[]{:T(128)S(6)} %select_n.23), kind=kOutput, calls=%fused_computation.168 | convolution fusion | flops 201457664 | bytes 2228228 | tf_op jit(solution)/shard_map/dot_general | solution.py:21
  52.3 1.6 %collective-permute-start.20 = (f32[128,1024]{1,0:T(8,128)S(1)}, f32[128,1024]{1,0:T(8,128)S(1)}, u32[]{:S(2)}, u32[]{:S(2)}) collective-permute-start(f32[128,1024]{1,0:T(8,128)S(1)} %convolution_add_fusion.18), channel_id=1, source_target_pairs={{0,16},{8,24},{16,0},{24,8},{1,17},{9,25},{17,1},{25,9},{2,18},{10... | collective-permute-start | bytes 1572872 | tf_op jit(solution)/shard_map/ppermute | solution.py:17
  53.9 3.8 %fusion.154 = f32[128,1024]{1,0:T(8,128)S(1)} fusion(f32[128,1024]{1,0:T(8,128)S(1)} %fusion.151, f32[1024]{0:T(1024)S(1)} %bitcast.174, f32[1024]{0:T(1024)S(1)} %bitcast.175, f32[1024]{0:T(1024)S(1)} %bitcast.173, f32[1024]{0:T(1024)S(1)} %bitcast.171, f32[1024]{0:T(1024)S(1)} %bitcast.168, f32[1024]{0:T(1024)S(1)} %bitcast.165, ...), kind=kOutput, calls=%fused_computation.172 | convolution fusion | flops 816054272 | bytes 1597444 | tf_op jit(solution)/shard_map/dot_general | solution.py:21
  57.7 3.8 %collective-permute-done.22 = f32[131,1024]{1,0:T(8,128)S(1)} collective-permute-done((f32[131,1024]{1,0:T(8,128)}, f32[131,1024]{1,0:T(8,128)S(1)}, u32[]{:S(2)}, u32[]{:S(2)}) %collective-permute-start.22) | collective-permute-done | bytes 536608 | tf_op jit(solution)/shard_map/ppermute | solution.py:71
  61.5 4.0 %collective-permute-done.20 = f32[128,1024]{1,0:T(8,128)S(1)} collective-permute-done((f32[128,1024]{1,0:T(8,128)S(1)}, f32[128,1024]{1,0:T(8,128)S(1)}, u32[]{:S(2)}, u32[]{:S(2)}) %collective-permute-start.20) | collective-permute-done | bytes 524320 | tf_op jit(solution)/shard_map/ppermute | solution.py:17
  65.5 1.6 %fusion.150 = f32[128,1024]{1,0:T(8,128)S(1)} fusion(f32[128,1024]{1,0:T(8,128)S(1)} %collective-permute-done.20, f32[128,1024]{1,0:T(8,128)S(1)} %fusion.167, f32[128,256]{1,0:T(8,128)S(1)} %collective-permute-done.18, f32[256,4096]{1,0:T(8,128)} %collective-permute-done.19, s32[]{:T(128)S(6)} %select_n.22), kind=kOutput, calls=%fused_computation.170 | convolution fusion | flops 201588736 | bytes 2752516 | tf_op jit(solution)/shard_map/dot_general | solution.py:21
  67.2 3.6 %fusion.160 = f32[128,1024]{1,0:T(8,128)} fusion(f32[128,1024]{1,0:T(8,128)S(1)} %fusion.150, f32[128,1024]{1,0:T(8,128)S(1)} %fusion.154, f32[1024]{0:T(1024)S(1)} %bitcast.177, f32[1024]{0:T(1024)S(1)} %bitcast.178, f32[1024]{0:T(1024)S(1)} %bitcast.176, f32[1024]{0:T(1024)S(1)} %bitcast.172, f32[1024]{0:T(1024)S(1)} %bitcast.169, ...), kind=kOutput, calls=%fused_computation.174 | convolution fusion | flops 816185344 | bytes 2121732 | tf_op jit(solution)/shard_map/dot_general | solution.py:21
  (4 shorter events, 0.1 us)
Async XLA Ops:
  0.0 5.3 %copy-start = (f32[1024,256]{1,0:T(8,128)S(1)}, f32[1024,256]{1,0:T(8,128)}, u32[]{:S(2)}) copy-start(f32[1024,256]{1,0:T(8,128)} %param.23) | copy-start | bytes 3145732
  0.0 50.6 %collective-permute-start.19 = (f32[256,4096]{1,0:T(8,128)}, f32[256,4096]{1,0:T(8,128)}, u32[]{:S(2)}, u32[]{:S(2)}) collective-permute-start(f32[256,4096]{1,0:T(8,128)} %param.26), channel_id=1, source_target_pairs={{0,8},{8,0},{16,24},{24,16},{1,9},{9,1},{17,25},{25,17},{2,10},{10... | collective-permute-start | bytes 12582920 | tf_op jit(solution)/shard_map/ppermute | solution.py:17
  6.8 24.6 %copy-start.1 = (f32[128,1024]{1,0:T(8,128)S(1)}, f32[128,1024]{1,0:T(8,128)}, u32[]{:S(2)}) copy-start(f32[128,1024]{1,0:T(8,128)} %param.19) | copy-start | bytes 1572868
  6.8 24.6 %copy-start.2 = (f32[3,1024]{1,0:T(4,128)S(1)}, f32[3,1024]{1,0:T(4,128)}, u32[]{:S(2)}) copy-start(f32[3,1024]{1,0:T(4,128)} %param.20) | copy-start | bytes 36868
  6.8 26.0 %copy-start.3 = (s32[1,2]{1,0:T(1,128)S(1)}, s32[1,2]{1,0:T(1,128)}, u32[]{:S(2)}) copy-start(s32[1,2]{1,0:T(1,128)} %param.21) | copy-start | bytes 28
  6.9 6.8 %collective-permute-start.9 = (f32[128,256]{1,0:T(8,128)S(1)}, f32[128,256]{1,0:T(8,128)S(1)}, u32[]{:S(2)}, u32[]{:S(2)}) collective-permute-start(f32[128,256]{1,0:T(8,128)S(1)} %get-tuple-element.57), channel_id=1, source_target_pairs={{0,2},{1,3},{2,0},{3,1},{4,6},{5,7},{6,4},{7,5},{8,10},{9,11},{10,... | collective-permute-start | bytes 393224 | tf_op jit(solution)/shard_map/cond/branch_3_fun/ppermute | solution.py:17
  14.8 9.0 %collective-permute-start.10 = (f32[128,256]{1,0:T(8,128)S(1)}, f32[128,256]{1,0:T(8,128)S(1)}, u32[]{:S(2)}, u32[]{:S(2)}) collective-permute-start(f32[128,256]{1,0:T(8,128)S(1)} %convolution_add_fusion.11), channel_id=1, source_target_pairs={{0,4},{1,5},{2,6},{3,7},{4,0},{5,1},{6,2},{7,3},{8,12},{9,13},{10,... | collective-permute-start | bytes 393224 | tf_op jit(solution)/shard_map/cond/branch_3_fun/ppermute | solution.py:17
  25.0 5.0 %collective-permute-start.11 = (f32[128,256]{1,0:T(8,128)S(1)}, f32[128,256]{1,0:T(8,128)S(1)}, u32[]{:S(2)}, u32[]{:S(2)}) collective-permute-start(f32[128,256]{1,0:T(8,128)S(1)} %convolution_add_fusion.10), channel_id=1, source_target_pairs={{0,1},{1,0},{2,3},{3,2},{4,5},{5,4},{6,7},{7,6},{8,9},{9,8},{10,11... | collective-permute-start | bytes 393224 | tf_op jit(solution)/shard_map/cond/branch_3_fun/ppermute | solution.py:17
  31.3 19.3 %collective-permute-start.18 = (f32[128,256]{1,0:T(8,128)S(1)}, f32[128,256]{1,0:T(8,128)S(1)}, u32[]{:S(2)}, u32[]{:S(2)}) collective-permute-start(f32[128,256]{1,0:T(8,128)S(1)} %get-tuple-element.82), channel_id=1, source_target_pairs={{0,8},{8,0},{16,24},{24,16},{1,9},{9,1},{17,25},{25,17},{2,10},{10... | collective-permute-start | bytes 393224 | tf_op jit(solution)/shard_map/ppermute | solution.py:17
  31.4 15.2 %collective-permute-start.21 = (f32[131,1024]{1,0:T(8,128)S(1)}, f32[131,1024]{1,0:T(8,128)}, u32[]{:S(2)}, u32[]{:S(2)}) collective-permute-start(f32[131,1024]{1,0:T(8,128)S(1)} %pad_maximum_fusion), channel_id=1, source_target_pairs={{0,1},{1,0},{2,3},{3,2},{4,5},{5,4},{6,7},{7,6},{8,9},{9,8},{10,11... | collective-permute-start | bytes 1609736 | tf_op jit(solution)/shard_map/ppermute | solution.py:17
  46.6 14.9 %collective-permute-start.22 = (f32[131,1024]{1,0:T(8,128)}, f32[131,1024]{1,0:T(8,128)S(1)}, u32[]{:S(2)}, u32[]{:S(2)}) collective-permute-start(f32[131,1024]{1,0:T(8,128)} %collective-permute-done.21), channel_id=1, source_target_pairs={{0,2},{2,4},{4,6},{3,1},{5,3},{7,5},{8,10},{10,12},{12,14},{11,9},... | collective-permute-start | bytes 1609736 | tf_op jit(solution)/shard_map/ppermute | solution.py:71
  52.3 13.2 %collective-permute-start.20 = (f32[128,1024]{1,0:T(8,128)S(1)}, f32[128,1024]{1,0:T(8,128)S(1)}, u32[]{:S(2)}, u32[]{:S(2)}) collective-permute-start(f32[128,1024]{1,0:T(8,128)S(1)} %convolution_add_fusion.18), channel_id=1, source_target_pairs={{0,16},{8,24},{16,0},{24,8},{1,17},{9,25},{17,1},{25,9},{2,18},{10... | collective-permute-start | bytes 1572872 | tf_op jit(solution)/shard_map/ppermute | solution.py:17
